TPU v7x, 128 devices: a whole 4x4x4 slice. The times are simulated.
128 devices in a mesh: row: 8 (over y_lo, x), col: 16 (over z, y_hi, core).
Axes of the slice: x: 4, y: 4 (y_hi: 2, y_lo: 2; y = y_hi * 2 + y_lo), z: 4, core: 2. Of those that a mesh axis runs over, the one named last changes fastest.
Arguments:
- points: bfloat16 [64, 65536], P(None, ('row', 'col')), may hold values from -6 to 6
- solution: float32 [16, 65536], P(None, ('row', 'col')), may hold values from -6 to 6
- residual: float32 [16, 65536], P(None, ('row', 'col')), may hold values from -6 to 6
- direction: float32 [16, 65536], P(None, ('row', 'col')), may hold values from -6 to 6
Outputs:
- solution_next: float32 [16, 65536], P(None, ('row', 'col'))
- residual_next: float32 [16, 65536], P(None, ('row', 'col'))
- direction_next: float32 [16, 65536], P(None, ('row', 'col'))
All inputs are finite; a program needn't handle non-finite values.
Results may differ from a plain program's by a relative error of at most 0.0042.
Values may be sent and summed in bfloat16 or wider, within the bound.
A program may use at most 64 MiB of HBM per device.

v0:
```python
import jax
import jax.numpy as jnp
import numpy as np
from jax import lax
from jax.sharding import PartitionSpec as P

F = 64
TILE = 2048


def pair_table(tile_count, device_count):
    pairs = [(i, j) for i in range(tile_count) for j in range(i, tile_count)]
    slot_count = (len(pairs) + device_count - 1) // device_count
    table = np.full((device_count, slot_count, 2), tile_count, np.int32)
    for position, pair in enumerate(pairs):
        table[position % device_count, position // device_count, 0] = pair[0]
        table[position % device_count, position // device_count, 1] = pair[1]
    return table


def add_columns(accumulated, column_start, piece):
    current = lax.dynamic_slice_in_dim(accumulated, column_start, piece.shape[1], 1)
    return lax.dynamic_update_slice_in_dim(accumulated, current + piece, column_start, 1)


def triangle_terms(everyone, sq_norms, all_directions, my_pairs):
    total_points = everyone.shape[1]
    tile_count = total_points // TILE
    block_rows = min(512, TILE)

    def one_pair(slot_index, accumulated):
        row_tile = my_pairs[slot_index, 0]
        col_tile = my_pairs[slot_index, 1]
        slot_live = row_tile < tile_count
        weight = slot_live.astype(jnp.float32)
        mirror = weight * (row_tile != col_tile).astype(jnp.float32)
        row_base = (jnp.minimum(row_tile, tile_count - 1) * TILE).astype(jnp.int32)
        col_start = (jnp.minimum(col_tile, tile_count - 1) * TILE).astype(jnp.int32)
        col_points = lax.dynamic_slice_in_dim(everyone, col_start, TILE, 1)
        col_norms = lax.dynamic_slice_in_dim(sq_norms, col_start, TILE, 0)
        col_vectors = lax.dynamic_slice_in_dim(all_directions, col_start, TILE, 1)
        mirrored = jnp.zeros((all_directions.shape[0], TILE), jnp.float32)
        for piece_index in range(TILE // block_rows):
            row_start = row_base + piece_index * block_rows
            row_points = lax.dynamic_slice_in_dim(everyone, row_start, block_rows, 1)
            row_norms = lax.dynamic_slice_in_dim(sq_norms, row_start, block_rows, 0)
            row_vectors = lax.dynamic_slice_in_dim(all_directions, row_start, block_rows, 1)
            cross_terms = lax.dot_general(
                row_points, col_points, (((0,), (0,)), ((), ())), preferred_element_type=jnp.float32
            )
            dist = row_norms[:, None] + col_norms[None, :] - 2.0 * cross_terms
            kernel = jnp.exp(-(2.0 / F) * dist).astype(jnp.bfloat16)
            row_terms = lax.dot_general(
                col_vectors, kernel, (((1,), (1,)), ((), ())), preferred_element_type=jnp.float32
            )
            accumulated = add_columns(accumulated, row_start, weight * row_terms)
            mirrored = mirrored + jnp.dot(row_vectors, kernel, preferred_element_type=jnp.float32)
        return add_columns(accumulated, col_start, mirror * mirrored)

    return lax.fori_loop(
        0,
        my_pairs.shape[0],
        one_pair,
        jnp.zeros((all_directions.shape[0], total_points), jnp.float32),
    )


def on_device(points, solution, residual, direction):
    local_width = points.shape[1]
    everyone = lax.all_gather(points, ("row", "col"), axis=1, tiled=True)
    total_points = everyone.shape[1]
    tile_count = total_points // TILE
    sq_norms = jnp.sum(jnp.square(everyone.astype(jnp.float32)), axis=0)
    all_directions = lax.all_gather(
        direction.astype(jnp.bfloat16), ("row", "col"), axis=1, tiled=True
    )
    table = jnp.asarray(pair_table(tile_count, lax.axis_size(("row", "col"))))
    my_pairs = table[lax.axis_index(("row", "col"))]
    accumulated = triangle_terms(everyone, sq_norms, all_directions, my_pairs)
    summed = lax.psum(accumulated, ("row", "col"))
    own_start = lax.axis_index(("row", "col")) * local_width
    own_rows = lax.dynamic_slice_in_dim(summed, own_start, local_width, 1)
    image_rows = 1.0 * direction + own_rows
    old_norm = lax.psum(jnp.sum(residual * residual, axis=1), ("row", "col"))
    curvature = lax.psum(jnp.sum(direction * image_rows, axis=1), ("row", "col"))
    step_size = old_norm / curvature
    residual_next = residual - step_size[:, None] * image_rows
    new_norm = lax.psum(jnp.sum(residual_next * residual_next, axis=1), ("row", "col"))
    solution_next = solution + step_size[:, None] * direction
    direction_next = residual_next + (new_norm / old_norm)[:, None] * direction
    return (solution_next, residual_next, direction_next)


def solution(mesh):
    placed = (
        P(None, ("row", "col")),
        P(None, ("row", "col")),
        P(None, ("row", "col")),
        P(None, ("row", "col")),
    )
    return jax.shard_map(
        on_device,
        mesh=mesh,
        in_specs=placed,
        out_specs=(P(None, ("row", "col")), P(None, ("row", "col")), P(None, ("row", "col"))),
        check_vma=False,
    )
```

profile of v0, /device:TPU:1, one launch (start us, length us, event | category | flops | bytes accessed | tf_op | source)
XLA Modules:
  0.0 835.4 jit_solution(7481728378052199383)
XLA Ops:
  10.1 204.3 %all-gather.5.cloned.1.call-done = bf16[64,65536]{1,0:T(8,128)(2,1)} async-done(((bf16[64,512]{1,0:T(8,128)(2,1)}), bf16[64,65536]{1,0:T(8,128)(2,1)}) %all-gather.5.cloned.1.call-update) | async-done | bytes 8388624 | tf_op jit(solution)/shard_map/all_gather | solution.py:70
  214.4 5.5 multiply_reduce_fusion
  219.9 191.2 %all-gather.3.cloned.1.call-done = bf16[16,65536]{1,0:T(8,128)(2,1)} async-done(((bf16[16,512]{1,0:T(8,128)(2,1)}), bf16[16,65536]{1,0:T(8,128)(2,1)}) %all-gather.3.cloned.1.call-update) | async-done | bytes 2097168 | tf_op jit(solution)/shard_map/all_gather | solution.py:74
  411.0 2.2 broadcast_in_dim.24
  413.3 131.7 %while.15 = (s32[]{:T(128)}, f32[16,65536]{1,0:T(8,128)}, s32[5,2]{0,1:T(2,128)S(1)}, bf16[16,65536]{1,0:T(8,128)(2,1)}, f32[65536]{0:T(1024)S(1)}, /*index=5*/b...) while((s32[]{:T(128)}, f32[16,65536]{1,0:T(8,128)}, ...), condition=%wide.region_4.0_spmd, body=%wide.region_3.0_spmd.sunk | while | flops 826507264 | bytes 28191316 | solution.py:60
  417.3 2.1 exponential_convert_fusion.8
  420.5 2.1 fusion.105
  422.6 2.1 exponential_convert_fusion.9
  425.9 2.1 fusion.106
  428.0 2.1 exponential_convert_fusion.10
  431.2 2.1 fusion.107
  433.4 2.1 exponential_convert_fusion.11
  435.5 2.1 fusion.108
  443.6 2.1 exponential_convert_fusion.8
  446.8 2.1 fusion.105
  448.9 2.1 exponential_convert_fusion.9
  452.2 2.1 fusion.106
  454.3 2.1 exponential_convert_fusion.10
  457.6 2.1 fusion.107
  459.7 2.1 exponential_convert_fusion.11
  461.8 2.1 fusion.108
  469.9 2.1 exponential_convert_fusion.8
  473.1 2.1 fusion.105
  475.2 2.1 exponential_convert_fusion.9
  478.5 2.1 fusion.106
  480.6 2.1 exponential_convert_fusion.10
  483.9 2.1 fusion.107
  486.0 2.1 exponential_convert_fusion.11
  488.1 2.1 fusion.108
  496.2 2.1 exponential_convert_fusion.8
  499.4 2.1 fusion.105
  501.6 2.1 exponential_convert_fusion.9
  504.8 2.1 fusion.106
  506.9 2.1 exponential_convert_fusion.10
  510.2 2.1 fusion.107
  512.3 2.1 exponential_convert_fusion.11
  514.4 2.1 fusion.108
  522.4 2.2 exponential_convert_fusion.8
  525.7 2.1 fusion.105
  527.9 2.2 exponential_convert_fusion.9
  531.2 2.1 fusion.106
  533.3 2.2 exponential_convert_fusion.10
  536.6 2.1 fusion.107
  538.7 2.2 exponential_convert_fusion.11
  540.9 2.1 fusion.108
  545.8 152.4 %all-reduce.3.cloned.1.call-done = f32[16,65536]{1,0:T(8,128)} async-done(((f32[16,65536]{1,0:T(8,128)}), f32[16,65536]{1,0:T(8,128)}) %all-reduce.3.cloned.1.call-update) | async-done | bytes 4194320 | tf_op jit(solution)/shard_map/psum | solution.py:80
  699.1 64.0 %all-reduce = (f32[16]{0:T(128)S(1)}, f32[16]{0:T(128)S(1)}) all-reduce(f32[16]{0:T(128)S(1)} %multiply_reduce_fusion.3, f32[16]{0:T(128)S(1)} %multiply_reduce_fusion.2), channel_id=1, replica_groups=mesh['row'=8,'col'=16] {'row','col'}, use_global_device_ids=true, to_apply=%region_1.0 | all-reduce | flops 32 | bytes 256 | tf_op jit(solution)/shard_map/psum | solution.py:84
  764.6 63.5 %psum.31 = f32[16]{0:T(128)S(1)} all-reduce(f32[16]{0:T(128)S(1)} %get-tuple-element.174), channel_id=1, replica_groups=mesh['row'=8,'col'=16] {'row','col'}, use_global_device_ids=true, to_apply=%region_9.0 | all-reduce | flops 16 | bytes 128 | tf_op jit(solution)/shard_map/psum | solution.py:88
  (57 shorter events, 36.8 us)
Async XLA Ops:
  7.2 207.2 %all-gather.5.cloned.1.call-start = ((), (), s32[]{:S(2)}) async-start(), calls=%async_computation.1 | async-start | bytes 8454144 | tf_op jit(solution)/shard_map/all_gather | solution.py:70
  7.9 403.1 %all-gather.3.cloned.1.call-start = ((), (), s32[]{:S(2)}) async-start(), calls=%async_computation | async-start | bytes 2113536 | tf_op jit(solution)/shard_map/all_gather | solution.py:74
  9.3 688.9 %all-reduce.3.cloned.1.call-start = ((), (), s32[]{:S(2)}) async-start(), calls=%async_computation.2 | async-start | bytes 8388608 | tf_op jit(solution)/shard_map/psum | solution.py:80
  545.0 0.8 copy-start.2
  545.0 153.2 %copy-start = (f32[16,512]{1,0:T(8,128)S(1)}, f32[16,512]{1,0:T(8,128)}, u32[]{:S(2)}) copy-start(f32[16,512]{1,0:T(8,128)} %param.10) | copy-start | bytes 98308
  545.0 218.1 %copy-start.3 = (f32[16,512]{1,0:T(8,128)S(1)}, f32[16,512]{1,0:T(8,128)}, u32[]{:S(2)}) copy-start(f32[16,512]{1,0:T(8,128)} %param.8) | copy-start | bytes 98308
  764.6 64.2 %copy-start.1 = (f32[16,512]{1,0:T(8,128)}, f32[16,512]{1,0:T(8,128)S(1)}, u32[]{:S(2)}) copy-start(f32[16,512]{1,0:T(8,128)S(1)} %get-tuple-element.175) | copy-start | bytes 98308
Sparse Core Ops, SparseCore 0:
  9.7 204.6 all-gather.4
  216.7 194.2 all-gather.2
  545.1 153.0 all-reduce.2
where the time goes:
time: 838 us; the launch traced here: 835 us
  waiting for transfers between devices  549 us (66%)
  blocking collectives  128 us (15%)
  matrix products  112 us (13%)
  loops' own time  16.6 us (2%)
  between operations  13.8 us (2%)
  other arithmetic  10.1 us (1%)
    all_gather x1, waiting for transfers between devices, on_device(): everyone = lax.all_gather(points, ('row', 'col'), axis=1, tiled=True)  204 us
    all_gather x1, waiting for transfers between devices, on_device(): lax.all_gather(direction.astype(jnp.bfloat16), ('row', 'col'), axis=1, ti...  191 us
    psum x1, waiting for transfers between devices, on_device(): summed = lax.psum(accumulated, ('row', 'col'))  152 us
    psum x1, blocking collectives, on_device(): old_norm = lax.psum(jnp.sum(residual * residual, axis=1), ('row', 'col'))  64 us
    psum x1, blocking collectives, on_device(): lax.psum(jnp.sum(residual_next * residual_next, axis=1), ('row', 'col'))  63.5 us
    dot_general x20, matrix products, one_pair(): lax.dot_general(row_points, col_points, (((0,), (0,)), ((), ())), preferr...  42.8 us
    dot_general x20, matrix products, one_pair(): lax.dot_general(col_vectors, kernel, (((1,), (1,)), ((), ())), preferred_...  42.4 us
    dot_general x20, matrix products, one_pair(): jnp.dot(row_vectors, kernel, preferred_element_type=jnp.float32)  26.5 us
  transfers between devices with their start and end apart: 3, of which 3 were waited for; matrix products, arithmetic and copies ran while one was open for 1% of the time, Pallas kernels for 0%

commit v1 on v0

--- a/solution.py
+++ b/solution.py
@@ -81,7 +81,7 @@
     own_start = lax.axis_index(("row", "col")) * local_width
     own_rows = lax.dynamic_slice_in_dim(summed, own_start, local_width, 1)
     image_rows = 1.0 * direction + own_rows
-    old_norm = lax.psum(jnp.sum(residual * residual, axis=1), ("row", "col"))
+    old_norm = lax.psum(lax.psum(jnp.sum(residual * residual, axis=1), "row"), "col")
     curvature = lax.psum(jnp.sum(direction * image_rows, axis=1), ("row", "col"))
     step_size = old_norm / curvature
     residual_next = residual - step_size[:, None] * image_rows

time: 838 us -> 874 us (1.043)
  blocking collectives: 128 us -> 177 us
  waiting for transfers between devices: 549 us -> 534 us
    psum x1 -> x3, blocking collectives: 64 us -> 113 us  [the longest x1 65.1 us: on_device(): lax.psum(jnp.sum(direction * image_rows, axis=1), ('row', 'col'))]
    psum x1, waiting for transfers between devices: 152 us -> 138 us  [on_device(): summed = lax.psum(accumulated, ('row', 'col'))]
where the time goes in v1:
time: 874 us; the launch traced here: 871 us
  waiting for transfers between devices  534 us (61%)
  blocking collectives  177 us (20%)
  matrix products  112 us (13%)
  loops' own time  16.6 us (2%)
  between operations  13.8 us (2%)
  other arithmetic  10.1 us (1%)
    all_gather x1, waiting for transfers between devices, on_device(): everyone = lax.all_gather(points, ('row', 'col'), axis=1, tiled=True)  204 us
    all_gather x1, waiting for transfers between devices, on_device(): lax.all_gather(direction.astype(jnp.bfloat16), ('row', 'col'), axis=1, ti...  191 us
    psum x1, waiting for transfers between devices, on_device(): summed = lax.psum(accumulated, ('row', 'col'))  138 us
    psum x1, blocking collectives, on_device(): lax.psum(jnp.sum(direction * image_rows, axis=1), ('row', 'col'))  65.1 us
    psum x1, blocking collectives, on_device(): lax.psum(jnp.sum(residual_next * residual_next, axis=1), ('row', 'col'))  64.5 us
    dot_general x20, matrix products, one_pair(): lax.dot_general(row_points, col_points, (((0,), (0,)), ((), ())), preferr...  42.8 us
    dot_general x20, matrix products, one_pair(): lax.dot_general(col_vectors, kernel, (((1,), (1,)), ((), ())), preferred_...  42.4 us
    psum x1, blocking collectives, on_device(): lax.psum(lax.psum(jnp.sum(residual * residual, axis=1), 'row'), 'col')  33.3 us
  transfers between devices with their start and end apart: 3, of which 3 were waited for; matrix products, arithmetic and copies ran while one was open for 1% of the time, Pallas kernels for 0%

profile of v1, /device:TPU:1, one launch (start us, length us, event | category | flops | bytes accessed | tf_op | source)
XLA Modules:
  0.0 870.7 jit_solution(10551778308989431752)
XLA Ops:
  10.1 204.3 %all-gather.5.cloned.1.call-done = bf16[64,65536]{1,0:T(8,128)(2,1)} async-done(((bf16[64,512]{1,0:T(8,128)(2,1)}), bf16[64,65536]{1,0:T(8,128)(2,1)}) %all-gather.5.cloned.1.call-update) | async-done | bytes 8388624 | tf_op jit(solution)/shard_map/all_gather | solution.py:70
  214.4 5.5 multiply_reduce_fusion
  219.9 191.2 %all-gather.3.cloned.1.call-done = bf16[16,65536]{1,0:T(8,128)(2,1)} async-done(((bf16[16,512]{1,0:T(8,128)(2,1)}), bf16[16,65536]{1,0:T(8,128)(2,1)}) %all-gather.3.cloned.1.call-update) | async-done | bytes 2097168 | tf_op jit(solution)/shard_map/all_gather | solution.py:74
  411.0 2.2 broadcast_in_dim.24
  413.3 131.7 %while.15 = (s32[]{:T(128)}, f32[16,65536]{1,0:T(8,128)}, s32[5,2]{0,1:T(2,128)S(1)}, bf16[16,65536]{1,0:T(8,128)(2,1)}, f32[65536]{0:T(1024)S(1)}, /*index=5*/b...) while((s32[]{:T(128)}, f32[16,65536]{1,0:T(8,128)}, ...), condition=%wide.region_5.0_spmd, body=%wide.region_4.0_spmd.sunk | while | flops 826507264 | bytes 28191316 | solution.py:60
  417.3 2.1 exponential_convert_fusion.8
  420.5 2.1 fusion.105
  422.6 2.1 exponential_convert_fusion.9
  425.9 2.1 fusion.106
  428.0 2.1 exponential_convert_fusion.10
  431.2 2.1 fusion.107
  433.4 2.1 exponential_convert_fusion.11
  435.5 2.1 fusion.108
  443.6 2.1 exponential_convert_fusion.8
  446.8 2.1 fusion.105
  448.9 2.1 exponential_convert_fusion.9
  452.2 2.1 fusion.106
  454.3 2.1 exponential_convert_fusion.10
  457.6 2.1 fusion.107
  459.7 2.1 exponential_convert_fusion.11
  461.8 2.1 fusion.108
  469.9 2.1 exponential_convert_fusion.8
  473.1 2.1 fusion.105
  475.2 2.1 exponential_convert_fusion.9
  478.5 2.1 fusion.106
  480.6 2.1 exponential_convert_fusion.10
  483.9 2.1 fusion.107
  486.0 2.1 exponential_convert_fusion.11
  488.1 2.1 fusion.108
  496.2 2.1 exponential_convert_fusion.8
  499.4 2.1 fusion.105
  501.6 2.1 exponential_convert_fusion.9
  504.8 2.1 fusion.106
  506.9 2.1 exponential_convert_fusion.10
  512.3 2.1 exponential_convert_fusion.11
  522.4 2.2 exponential_convert_fusion.8
  525.7 2.1 fusion.105
  527.9 2.2 exponential_convert_fusion.9
  531.2 2.1 fusion.106
  533.3 2.2 exponential_convert_fusion.10
  536.6 2.1 fusion.107
  538.7 2.2 exponential_convert_fusion.11
  540.9 2.1 fusion.108
  545.8 14.4 %psum.35 = f32[16]{0:T(128)S(1)} all-reduce(f32[16]{0:T(128)S(1)} %multiply_reduce_fusion.3), channel_id=1, replica_groups=mesh['row'=8,'col'=16] {'row'}, use_global_device_ids=true, to_apply=%region_1.0 | all-reduce | flops 16 | bytes 128 | tf_op jit(solution)/shard_map/psum | solution.py:84
  560.2 138.0 %all-reduce.2.cloned.1.call-done = f32[16,65536]{1,0:T(8,128)} async-done(((f32[16,65536]{1,0:T(8,128)}), f32[16,65536]{1,0:T(8,128)}) %all-reduce.2.cloned.1.call-update) | async-done | bytes 4194320 | tf_op jit(solution)/shard_map/psum | solution.py:80
  699.1 33.3 %psum.36 = f32[16]{0:T(128)S(1)} all-reduce(f32[16]{0:T(128)S(1)} %psum.35), channel_id=1, replica_groups=mesh['row'=8,'col'=16] {'col'}, use_global_device_ids=true, to_apply=%region_2.0 | all-reduce | flops 16 | bytes 128 | tf_op jit(solution)/shard_map/psum | solution.py:84
  732.3 65.1 %psum.38 = f32[16]{0:T(128)S(1)} all-reduce(f32[16]{0:T(128)S(1)} %multiply_reduce_fusion.2), channel_id=1, replica_groups=mesh['row'=8,'col'=16] {'row','col'}, use_global_device_ids=true, to_apply=%region_8.0 | all-reduce | flops 16 | bytes 128 | tf_op jit(solution)/shard_map/psum | solution.py:85
  799.0 64.5 %psum.39 = f32[16]{0:T(128)S(1)} all-reduce(f32[16]{0:T(128)S(1)} %get-tuple-element.172), channel_id=1, replica_groups=mesh['row'=8,'col'=16] {'row','col'}, use_global_device_ids=true, to_apply=%region_10.0 | all-reduce | flops 16 | bytes 128 | tf_op jit(solution)/shard_map/psum | solution.py:88
  (59 shorter events, 41.0 us)
Async XLA Ops:
  7.2 207.2 %all-gather.5.cloned.1.call-start = ((), (), s32[]{:S(2)}) async-start(), calls=%async_computation.1 | async-start | bytes 8454144 | tf_op jit(solution)/shard_map/all_gather | solution.py:70
  7.9 403.1 %all-gather.3.cloned.1.call-start = ((), (), s32[]{:S(2)}) async-start(), calls=%async_computation | async-start | bytes 2113536 | tf_op jit(solution)/shard_map/all_gather | solution.py:74
  9.3 688.9 %all-reduce.2.cloned.1.call-start = ((), (), s32[]{:S(2)}) async-start(), calls=%async_computation.2 | async-start | bytes 8388608 | tf_op jit(solution)/shard_map/psum | solution.py:80
  545.0 0.8 copy-start.2
  545.0 153.2 %copy-start = (f32[16,512]{1,0:T(8,128)S(1)}, f32[16,512]{1,0:T(8,128)}, u32[]{:S(2)}) copy-start(f32[16,512]{1,0:T(8,128)} %param.10) | copy-start | bytes 98308
  545.0 252.4 %copy-start.3 = (f32[16,512]{1,0:T(8,128)S(1)}, f32[16,512]{1,0:T(8,128)}, u32[]{:S(2)}) copy-start(f32[16,512]{1,0:T(8,128)} %param.8) | copy-start | bytes 98308
  799.0 65.2 %copy-start.1 = (f32[16,512]{1,0:T(8,128)}, f32[16,512]{1,0:T(8,128)S(1)}, u32[]{:S(2)}) copy-start(f32[16,512]{1,0:T(8,128)S(1)} %get-tuple-element.173) | copy-start | bytes 98308
Sparse Core Ops, SparseCore 0:
  9.7 204.6 all-gather.4
  216.7 194.2 all-gather.2
  545.1 153.0 all-reduce.1

commit v2 on v0

--- a/solution.py
+++ b/solution.py
@@ -67,7 +67,10 @@
 
 def on_device(points, solution, residual, direction):
     local_width = points.shape[1]
-    everyone = lax.all_gather(points, ("row", "col"), axis=1, tiled=True)
+    everyone = jnp.concatenate(
+        lax.all_to_all(jnp.stack([points] * lax.axis_size(("row", "col"))), ("row", "col"), 0, 0),
+        axis=1,
+    )
     total_points = everyone.shape[1]
     tile_count = total_points // TILE
     sq_norms = jnp.sum(jnp.square(everyone.astype(jnp.float32)), axis=0)

time: 838 us -> 723 us (0.86)
  waiting for transfers between devices: 549 us -> 408 us
  local copies, waits for them, and re-layouts: 7.1 us -> 19.7 us
  starting transfers between devices: 0.12 us -> 12 us
    all_gather x1 -> x0, waiting for transfers between devices: 204 us -> none  [on_device(): everyone = lax.all_gather(points, ('row', 'col'), axis=1, tiled=True)]
    all_to_all x0 -> x1, waiting for transfers between devices: none -> 108 us  [on_device(): lax.all_to_all(jnp.stack([points] * lax.axis_size(('row', 'col'))), ('row...]
    all_gather x1, waiting for transfers between devices: 191 us -> 148 us  [on_device(): lax.all_gather(direction.astype(jnp.bfloat16), ('row', 'col'), axis=1, ti...]
    all_to_all x0 -> x1, starting transfers between devices: none -> 11.9 us  [on_device(): lax.all_to_all(jnp.stack([points] * lax.axis_size(('row', 'col'))), ('row...]
  transfers between devices with their start and end apart: 3 -> 3, of which waited for: 3 -> 3; matrix products, arithmetic and copies ran while one was open for 1% -> 2% of each run, Pallas kernels for 0% -> 0%
where the time goes in v2:
time: 723 us; the launch traced here: 720 us
  waiting for transfers between devices  408 us (56%)
  blocking collectives  128 us (18%)
  matrix products  112 us (15%)
  local copies, waits for them, and re-layouts  19.7 us (3%)
  loops' own time  16.6 us (2%)
  between operations  14.1 us (2%)
  starting transfers between devices  12 us (2%)
  other arithmetic  10.3 us (1%)
    psum x1, waiting for transfers between devices, on_device(): summed = lax.psum(accumulated, ('row', 'col'))  152 us
    all_gather x1, waiting for transfers between devices, on_device(): lax.all_gather(direction.astype(jnp.bfloat16), ('row', 'col'), axis=1, ti...  148 us
    all_to_all x1, waiting for transfers between devices, on_device(): lax.all_to_all(jnp.stack([points] * lax.axis_size(('row', 'col'))), ('row...  108 us
    psum x1, blocking collectives, on_device(): old_norm = lax.psum(jnp.sum(residual * residual, axis=1), ('row', 'col'))  64 us
    psum x1, blocking collectives, on_device(): lax.psum(jnp.sum(residual_next * residual_next, axis=1), ('row', 'col'))  63.5 us
    dot_general x20, matrix products, one_pair(): lax.dot_general(row_points, col_points, (((0,), (0,)), ((), ())), preferr...  43.1 us
    dot_general x20, matrix products, one_pair(): lax.dot_general(col_vectors, kernel, (((1,), (1,)), ((), ())), preferred_...  42.3 us
    dot_general x20, matrix products, one_pair(): jnp.dot(row_vectors, kernel, preferred_element_type=jnp.float32)  26.5 us
  transfers between devices with their start and end apart: 3, of which 3 were waited for; matrix products, arithmetic and copies ran while one was open for 2% of the time, Pallas kernels for 0%

profile of v2, /device:TPU:1, one launch (start us, length us, event | category | flops | bytes accessed | tf_op | source)
XLA Modules:
  0.0 719.8 jit_solution(15552554246238078453)
XLA Ops:
  7.2 5.1 stack.2
  12.3 11.9 %all-to-all-start = ((bf16[128,64,512]{2,1,0:T(8,128)(2,1)}), bf16[128,64,512]{2,1,0:T(8,128)(2,1)}, u32[]{:S(2)}, u32[]{:S(2)}) async-start(bf16[128,64,512]{2,1,0:T(8,128)(2,1)} %stack.2), calls=%async_computation | async-start | bytes 16777216 | tf_op jit(solution)/shard_map/all_to_all | solution.py:71
  25.7 107.5 %all-to-all-done = bf16[128,64,512]{2,1,0:T(8,128)(2,1)} async-done(((bf16[128,64,512]{2,1,0:T(8,128)(2,1)}), bf16[128,64,512]{2,1,0:T(8,128)(2,1)}, u32[]{:S(2)}, u32[]{:S(2)}) %all-to-all-start) | async-done | bytes 8388640 | tf_op jit(solution)/shard_map/all_to_all | solution.py:71
  133.2 6.4 multiply_reduce_fusion
  139.7 7.4 %copy.9 = bf16[128,8,8,512]{3,2,0,1:T(8,128)(2,1)} copy(bf16[128,8,8,512]{3,2,1,0:T(8,128)(2,1)} %bitcast.6) | data formatting | bytes 16777216 | tf_op jit(solution)/shard_map/reshape | solution.py:70
  147.1 147.7 %all-gather.2.cloned.1.call-done = bf16[16,65536]{1,0:T(8,128)(2,1)} async-done(((bf16[16,512]{1,0:T(8,128)(2,1)}), bf16[16,65536]{1,0:T(8,128)(2,1)}) %all-gather.2.cloned.1.call-update) | async-done | bytes 2097168 | tf_op jit(solution)/shard_map/all_gather | solution.py:77
  294.8 2.2 broadcast_in_dim.24
  297.1 131.9 %while.15 = (s32[]{:T(128)}, f32[16,65536]{1,0:T(8,128)}, s32[5,2]{0,1:T(2,128)S(1)}, bf16[16,65536]{1,0:T(8,128)(2,1)}, f32[65536]{0:T(1024)S(1)}, /*index=5*/b...) while((s32[]{:T(128)}, f32[16,65536]{1,0:T(8,128)}, ...), condition=%wide.region_4.0_spmd, body=%wide.region_3.0_spmd.sunk | while | flops 826507264 | bytes 28191316 | solution.py:60
  301.1 2.1 exponential_convert_fusion.8
  304.3 2.1 fusion.105
  306.4 2.1 exponential_convert_fusion.9
  309.7 2.1 fusion.106
  311.8 2.1 exponential_convert_fusion.10
  315.1 2.1 fusion.107
  317.2 2.1 exponential_convert_fusion.11
  319.3 2.1 fusion.108
  327.4 2.1 exponential_convert_fusion.8
  330.7 2.1 fusion.105
  332.8 2.1 exponential_convert_fusion.9
  336.0 2.1 fusion.106
  338.2 2.1 exponential_convert_fusion.10
  341.4 2.1 fusion.107
  343.6 2.1 exponential_convert_fusion.11
  353.7 2.1 exponential_convert_fusion.8
  357.0 2.1 fusion.105
  359.1 2.1 exponential_convert_fusion.9
  362.4 2.1 fusion.106
  364.5 2.1 exponential_convert_fusion.10
  367.8 2.1 fusion.107
  369.9 2.1 exponential_convert_fusion.11
  372.1 2.1 fusion.108
  380.1 2.1 exponential_convert_fusion.8
  383.4 2.1 fusion.105
  385.5 2.1 exponential_convert_fusion.9
  388.8 2.1 fusion.106
  390.9 2.1 exponential_convert_fusion.10
  396.2 2.1 exponential_convert_fusion.11
  406.4 2.2 exponential_convert_fusion.8
  409.7 2.1 fusion.105
  411.8 2.2 exponential_convert_fusion.9
  415.2 2.1 fusion.106
  417.3 2.2 exponential_convert_fusion.10
  420.6 2.1 fusion.107
  422.7 2.2 exponential_convert_fusion.11
  424.9 2.1 fusion.108
  429.9 152.4 %all-reduce.3.cloned.1.call-done = f32[16,65536]{1,0:T(8,128)} async-done(((f32[16,65536]{1,0:T(8,128)}), f32[16,65536]{1,0:T(8,128)}) %all-reduce.3.cloned.1.call-update) | async-done | bytes 4194320 | tf_op jit(solution)/shard_map/psum | solution.py:83
  583.2 64.0 %all-reduce = (f32[16]{0:T(128)S(1)}, f32[16]{0:T(128)S(1)}) all-reduce(f32[16]{0:T(128)S(1)} %multiply_reduce_fusion.3, f32[16]{0:T(128)S(1)} %multiply_reduce_fusion.2), channel_id=1, replica_groups=mesh['row'=8,'col'=16] {'row','col'}, use_global_device_ids=true, to_apply=%region_1.0 | all-reduce | flops 32 | bytes 256 | tf_op jit(solution)/shard_map/psum | solution.py:87
  648.7 63.5 %psum.31 = f32[16]{0:T(128)S(1)} all-reduce(f32[16]{0:T(128)S(1)} %get-tuple-element.174), channel_id=1, replica_groups=mesh['row'=8,'col'=16] {'row','col'}, use_global_device_ids=true, to_apply=%region_9.0 | all-reduce | flops 16 | bytes 128 | tf_op jit(solution)/shard_map/psum | solution.py:91
  (59 shorter events, 41.7 us)
Async XLA Ops:
  12.3 12.0 %copy-start = (f32[16,512]{1,0:T(8,128)S(1)}, f32[16,512]{1,0:T(8,128)}, u32[]{:S(2)}) copy-start(f32[16,512]{1,0:T(8,128)} %param.10) | copy-start | bytes 98308
  12.3 120.9 %all-to-all-start = ((bf16[128,64,512]{2,1,0:T(8,128)(2,1)}), bf16[128,64,512]{2,1,0:T(8,128)(2,1)}, u32[]{:S(2)}, u32[]{:S(2)}) async-start(bf16[128,64,512]{2,1,0:T(8,128)(2,1)} %stack.2), calls=%async_computation | async-start | bytes 16777216 | tf_op jit(solution)/shard_map/all_to_all | solution.py:71
  24.2 270.6 %all-gather.2.cloned.1.call-start = ((), (), s32[]{:S(2)}) async-start(), calls=%async_computation.1 | async-start | bytes 2113536 | tf_op jit(solution)/shard_map/all_gather | solution.py:77
  25.0 557.3 %all-reduce.3.cloned.1.call-start = ((), (), s32[]{:S(2)}) async-start(), calls=%async_computation.2 | async-start | bytes 8388608 | tf_op jit(solution)/shard_map/psum | solution.py:83
  429.0 0.8 copy-start.2
  429.0 218.2 %copy-start.3 = (f32[16,512]{1,0:T(8,128)S(1)}, f32[16,512]{1,0:T(8,128)}, u32[]{:S(2)}) copy-start(f32[16,512]{1,0:T(8,128)} %param.8) | copy-start | bytes 98308
  648.7 64.2 %copy-start.1 = (f32[16,512]{1,0:T(8,128)}, f32[16,512]{1,0:T(8,128)S(1)}, u32[]{:S(2)}) copy-start(f32[16,512]{1,0:T(8,128)S(1)} %get-tuple-element.175) | copy-start | bytes 98308
Sparse Core Ops, SparseCore 0:
  27.3 267.4 all-gather.1
  429.1 153.1 all-reduce.2
